TPU v7x, 32 devices: a whole 2x2x4 slice. The times are simulated.
32 devices in a mesh: tm: 8 (over y, x, core), strip: 4 (over z).
Axes of the slice: x: 2, y: 2, z: 4, core: 2. Of those that a mesh axis runs over, the one named last changes fastest.
Arguments:
- signal: bfloat16 [2, 16, 16384], P(None, 'strip', 'tm'), may hold values from -5 to 5
Outputs:
- spectrum: bfloat16 [2, 256, 16, 8, 2048], P(None, 'strip', None, 'tm')
All inputs are finite; a program needn't handle non-finite values.
Results may differ from a plain program's by a relative error of at most 0.0069.
Values may be sent and summed in bfloat16 or wider, within the bound.
A program may use at most 128 MiB of HBM per device.

v0:
```python
import math
import jax
import jax.numpy as jnp
from jax import lax
from jax.sharding import PartitionSpec as P

K = 256
TWO_PI = 2.0 * math.pi


def passed_along(value, axis, steps):
    count = lax.axis_size(axis)
    leading, last = (max(0, -steps), min(count, count - steps))
    return lax.ppermute(value, axis, [(source, source + steps) for source in range(leading, last)])


def channel_filters(channel_ids, length):
    offsets = jnp.arange(length, dtype=jnp.int32)
    phases = channel_ids[:, None] * offsets[None, :] % length
    angles = jnp.float32(TWO_PI) * phases.astype(jnp.float32) / length
    hamming = 0.54 - 0.46 * jnp.cos(jnp.float32(TWO_PI) * offsets.astype(jnp.float32) / length)
    scaled = hamming[None, :] / math.sqrt(length)
    cosine = scaled * jnp.cos(angles)
    sine = scaled * jnp.sin(angles)
    real_rows = jnp.stack([cosine, sine], axis=1)
    imag_rows = jnp.stack([-sine, cosine], axis=1)
    return jnp.concatenate([real_rows, imag_rows], axis=0).astype(jnp.bfloat16)


def dft_pair(first, second, modulus, norm):
    phases = first[:, None] * second[None, :] % modulus
    angles = jnp.float32(TWO_PI) * phases.astype(jnp.float32) / modulus
    return (jnp.cos(angles) * norm, jnp.sin(angles) * norm)


def channelize(extended, filters, channel_count, length):
    outcome = lax.conv_general_dilated(
        extended,
        filters,
        (1,),
        "VALID",
        dimension_numbers=("CNH", "OIH", "CNH"),
        preferred_element_type=jnp.float32,
    )
    window_count = extended.shape[1]
    spectra = outcome[:, :, :length].reshape(2, channel_count, window_count, length)
    centered = extended[:, :, K // 2 : K // 2 + length].astype(jnp.float32)
    real_part = spectra[0] * centered[0][None] + spectra[1] * centered[1][None]
    imag_part = spectra[1] * centered[0][None] - spectra[0] * centered[1][None]
    return jnp.stack([real_part, imag_part]).astype(jnp.bfloat16)


def first_pass(values):
    residues = lax.axis_size("tm")
    block_len = values.shape[2]
    piece_len = block_len // residues
    total_len = block_len * residues
    grouped = values.reshape(2, values.shape[1], residues, piece_len)
    res_ids = jnp.arange(residues, dtype=jnp.int32)
    small_cos, small_sin = dft_pair(res_ids, res_ids, residues, 1.0 / math.sqrt(residues))
    small_cos = small_cos.astype(jnp.bfloat16)
    small_sin = small_sin.astype(jnp.bfloat16)
    section_real = jnp.einsum(
        "qn,rns->rqs", small_cos, grouped[0], preferred_element_type=jnp.float32
    ) + jnp.einsum("qn,rns->rqs", small_sin, grouped[1], preferred_element_type=jnp.float32)
    section_imag = jnp.einsum(
        "qn,rns->rqs", small_cos, grouped[1], preferred_element_type=jnp.float32
    ) - jnp.einsum("qn,rns->rqs", small_sin, grouped[0], preferred_element_type=jnp.float32)
    sample_ids = lax.axis_index("tm") * piece_len + jnp.arange(piece_len, dtype=jnp.int32)
    twid_cos, twid_sin = dft_pair(res_ids, sample_ids, total_len, 1.0)
    turned_real = section_real * twid_cos[None] + section_imag * twid_sin[None]
    turned_imag = section_imag * twid_cos[None] - section_real * twid_sin[None]
    turned = jnp.stack([turned_real, turned_imag]).astype(jnp.bfloat16)
    return turned.reshape(2, values.shape[1], residues * piece_len)


def second_pass(values):
    block_len = values.shape[2]
    blk_ids = jnp.arange(block_len, dtype=jnp.int32)
    big_cos, big_sin = dft_pair(blk_ids, blk_ids, block_len, 1.0 / math.sqrt(block_len))
    big_cos = big_cos.astype(jnp.bfloat16)
    big_sin = big_sin.astype(jnp.bfloat16)
    out_real = jnp.dot(values[0], big_cos, preferred_element_type=jnp.float32) + jnp.dot(
        values[1], big_sin, preferred_element_type=jnp.float32
    )
    out_imag = jnp.dot(values[1], big_cos, preferred_element_type=jnp.float32) - jnp.dot(
        values[0], big_sin, preferred_element_type=jnp.float32
    )
    return jnp.stack([out_real, out_imag]).astype(jnp.bfloat16)


def per_device(signal):
    block_len = signal.shape[2]
    local_chan = K // lax.axis_size("strip")
    following = passed_along(signal[:, :, :K], "tm", -1)
    extended = jnp.concatenate([signal, following], axis=2)
    every_window = lax.all_gather(extended, "strip", axis=1, tiled=True)
    channel_ids = lax.axis_index("strip") * local_chan + jnp.arange(local_chan, dtype=jnp.int32)
    filters = channel_filters(channel_ids, K)
    products = channelize(every_window, filters, local_chan, block_len)
    window_total = products.shape[2]
    strips = products.reshape(2, local_chan * window_total, block_len)
    partial_sums = first_pass(lax.all_to_all(strips, "tm", split_axis=2, concat_axis=2, tiled=True))
    finished = second_pass(
        lax.all_to_all(partial_sums, "tm", split_axis=2, concat_axis=2, tiled=True)
    )
    return finished.reshape(2, local_chan, window_total, 1, block_len)


def solution(mesh):
    placed = (P(None, "strip", "tm"),)
    return jax.shard_map(
        per_device,
        mesh=mesh,
        in_specs=placed,
        out_specs=P(None, "strip", None, "tm", None),
        check_vma=False,
    )
```

profile of v0, /device:TPU:0, one launch (start us, length us, event | category | flops | bytes accessed | tf_op | source)
XLA Modules:
  0.0 851.7 jit_solution(14918469817403316897)
XLA Ops:
  4.6 15.4 %all_gather.3 = bf16[2,16,2304]{2,0,1:T(2,128)(2,1)S(1)} all-gather(bf16[2,4,2304]{2,0,1:T(2,128)(2,1)S(1)} %copy.40), channel_id=1, replica_groups=mesh['tm'=8,'strip'=4] {'strip'}, dimensions={1}, use_global_device_ids=true | all-gather | bytes 184320 | tf_op jit(solution)/shard_map/all_gather | solution.py:97
  24.6 135.8 %fusion.96 = f32[128,16,2048]{0,1,2:T(8,128)S(1)} fusion(bf16[2,16,2304]{1,0,2:T(2,128)(2,1)S(1)} %copy.41, bf16[128,2,256]{0,1,2:T(2,128)(2,1)S(1)} %copy.42), kind=kOutput, calls=%fused_computation.124 | convolution fusion | flops 4294967296 | bytes 17055744 | tf_op jit(solution)/shard_map/slice | solution.py:46
  160.4 16.4 %add_convert_fusion = (bf16[64,16,2048]{0,1,2:T(8,128)(2,1)}, bf16[64,16,2048]{0,1,2:T(8,128)(2,1)}) fusion(f32[128,16,2048]{0,1,2:T(8,128)S(1)} %fusion.96, f32[16,2048]{0,1:T(8,128)S(1)} %bitcast.78, f32[16,2048]{0,1:T(8,128)S(1)} %bitcast.77), kind=kLoop, calls=%fused_computation.11 | loop fusion | flops 16777216 | bytes 25427968 | tf_op jit(solution)/shard_map/convert.11
  176.8 12.0 %copy.45 = bf16[64,16,2048]{2,1,0:T(8,128)(2,1)} copy(bf16[64,16,2048]{0,1,2:T(8,128)(2,1)} %get-tuple-element.7) | data formatting | bytes 8388608 | tf_op jit(solution)/shard_map/convert.11
  188.8 12.1 %copy.46 = bf16[64,16,2048]{2,1,0:T(8,128)(2,1)} copy(bf16[64,16,2048]{0,1,2:T(8,128)(2,1)} %get-tuple-element.8) | data formatting | bytes 8388608 | tf_op jit(solution)/shard_map/convert.10
  200.9 7.6 pad_maximum_fusion
  208.5 21.4 %copy.47 = bf16[2,1024,2048]{1,0,2:T(2,128)(2,1)} copy(bf16[2,1024,2048]{2,1,0:T(8,128)(2,1)} %pad_maximum_fusion) | data formatting | bytes 16777216 | tf_op jit(solution)/shard_map/stack | solution.py:50
  235.2 94.0 %all-to-all-done = bf16[2,1024,2048]{1,0,2:T(2,128)(2,1)} async-done(((bf16[2,1024,2048]{1,0,2:T(2,128)(2,1)}), bf16[2,1024,2048]{1,0,2:T(2,128)(2,1)}, u32[]{:S(2)}, u32[]{:S(2)}) %all-to-all-start) | async-done | bytes 8388640 | tf_op jit(solution)/shard_map/all_to_all | solution.py:103
  329.1 17.4 %fusion.94 = (bf16[1,1024,2048]{1,0,2:T(2,128)(2,1)S(1)}, bf16[1,1024,2048]{1,0,2:T(2,128)(2,1)}) fusion(bf16[2,1024,2048]{1,0,2:T(2,128)(2,1)} %all-to-all-done), kind=kLoop, calls=%fused_computation.122 | loop fusion | bytes 16777216 | tf_op jit(solution)/shard_map/slice | solution.py:64
  350.3 6.9 copy.58
  357.2 6.9 fusion.45
  372.3 7.2 copy.59
  379.5 6.9 fusion.47
  386.4 15.8 %fusion.7 = (bf16[1024,8,256]{2,1,0:T(8,128)(2,1)}, bf16[1024,8,256]{2,1,0:T(8,128)(2,1)}) fusion(f32[8,256]{1,0:T(8,128)S(1)} %get-tuple-element.19, f32[8,256]{1,0:T(8,128)S(1)} %get-tuple-element.18, f32[1024,256,8]{1,2,0:T(8,128)} %fusion.45, f32[1024,256,8]{1,2,0:T(8,128)} %fusion.51, f32[1024,256,8]{1,2,0:T(8,128)} %fusion.47, ...), kind=kOutput, calls=%fused_computation.19 | convolution fusion | flops 54526976 | bytes 37765120 | tf_op jit(solution)/shard_map/qn,rns->rqs/dot_general | solution.py:66
  402.1 7.4 stack.44
  409.5 20.6 %copy.50 = bf16[1,1024,2048]{1,0,2:T(2,128)(2,1)} copy(bf16[1,1024,2048]{2,1,0:T(8,128)(2,1)} %stack.44) | data formatting | bytes 8388608 | tf_op jit(solution)/shard_map/stack | solution.py:73
  430.0 7.4 stack.45
  437.4 20.3 %copy.51 = bf16[1,1024,2048]{1,0,2:T(2,128)(2,1)} copy(bf16[1,1024,2048]{2,1,0:T(8,128)(2,1)} %stack.45) | data formatting | bytes 8388608 | tf_op jit(solution)/shard_map/stack | solution.py:73
  457.7 19.7 %pad_maximum_fusion.1 = bf16[2,1024,2048]{1,0,2:T(2,128)(2,1)} fusion(bf16[1,1024,2048]{1,0,2:T(2,128)(2,1)} %copy.51, bf16[1,1024,2048]{1,0,2:T(2,128)(2,1)} %copy.50), kind=kLoop, calls=%fused_computation.14 | loop fusion | flops 16777216 | bytes 16777216 | tf_op jit(solution)/shard_map/stack | solution.py:73
  477.4 5.2 all-to-all-start.1
  482.6 62.8 %multiply_convert_fusion.22 = bf16[2048,2048]{1,0:T(8,128)(2,1)} fusion(), kind=kLoop, calls=%fused_computation.7.clone.1.clone | loop fusion | flops 67108864 | bytes 8388608 | tf_op jit(solution)/shard_map/dot_general | solution.py:83
  545.4 63.3 %multiply_convert_fusion.20 = bf16[2048,2048]{1,0:T(8,128)(2,1)} fusion(), kind=kLoop, calls=%fused_computation.6.clone.1.clone.clone.clone.1 | loop fusion | flops 67108864 | bytes 8388608 | tf_op jit(solution)/shard_map/dot_general | solution.py:83
  608.7 62.8 %multiply_convert_fusion.21 = bf16[2048,2048]{1,0:T(8,128)(2,1)} fusion(), kind=kLoop, calls=%fused_computation.7.clone.clone.1 | loop fusion | flops 67108864 | bytes 8388608 | tf_op jit(solution)/shard_map/dot_general | solution.py:86
  671.5 63.3 %multiply_convert_fusion.19 = bf16[2048,2048]{1,0:T(8,128)(2,1)} fusion(), kind=kLoop, calls=%fused_computation.6.clone.clone.clone.clone.1 | loop fusion | flops 67108864 | bytes 8388608 | tf_op jit(solution)/shard_map/dot_general | solution.py:86
  734.8 17.6 %fusion.93 = (bf16[1,1024,2048]{1,0,2:T(2,128)(2,1)}, bf16[1,1024,2048]{1,0,2:T(2,128)(2,1)}) fusion(bf16[2,1024,2048]{1,0,2:T(2,128)(2,1)} %all-to-all-done.1), kind=kLoop, calls=%fused_computation.121 | loop fusion | bytes 16777216 | tf_op jit(solution)/shard_map/slice | solution.py:83
  752.4 20.1 %copy.62 = bf16[1,1024,2048]{2,1,0:T(8,128)(2,1)} copy(bf16[1,1024,2048]{1,0,2:T(2,128)(2,1)} %get-tuple-element.9) | data formatting | bytes 8388608
  772.5 19.8 %copy.63 = bf16[1,1024,2048]{2,1,0:T(8,128)(2,1)} copy(bf16[1,1024,2048]{1,0,2:T(2,128)(2,1)} %get-tuple-element.10) | data formatting | bytes 8388608
  792.3 14.9 %fusion.11 = f32[1024,2048]{1,0:T(8,128)} fusion(bf16[1,1024,2048]{2,1,0:T(8,128)(2,1)} %copy.62, bf16[2048,2048]{1,0:T(8,128)(2,1)} %multiply_convert_fusion.22), kind=kOutput, calls=%fused_computation.27 | convolution fusion | flops 8589934592 | bytes 20971520 | tf_op jit(solution)/shard_map/dot_general | solution.py:83
  807.2 13.3 %fusion.10 = f32[1024,2048]{1,0:T(8,128)} fusion(bf16[1,1024,2048]{2,1,0:T(8,128)(2,1)S(1)} %copy-done.2, bf16[2048,2048]{1,0:T(8,128)(2,1)} %multiply_convert_fusion.21), kind=kOutput, calls=%fused_computation.26 | convolution fusion | flops 8589934592 | bytes 20971520 | tf_op jit(solution)/shard_map/dot_general | solution.py:86
  820.5 12.1 %add_convert_fusion.1 = bf16[1024,2048]{1,0:T(8,128)(2,1)} fusion(f32[1024,2048]{1,0:T(8,128)} %fusion.11, bf16[1,1024,2048]{2,1,0:T(8,128)(2,1)S(1)} %copy-done.2, bf16[2048,2048]{1,0:T(8,128)(2,1)S(1)} %bitcast.76), kind=kOutput, calls=%fused_computation.25 | convolution fusion | flops 8594128896 | bytes 25165824 | tf_op jit(solution)/shard_map/dot_general | solution.py:83
  832.7 12.1 %subtract_convert_fusion.1 = bf16[1024,2048]{1,0:T(8,128)(2,1)} fusion(f32[1024,2048]{1,0:T(8,128)} %fusion.10, bf16[1,1024,2048]{2,1,0:T(8,128)(2,1)S(1)} %copy-done.1, bf16[2048,2048]{1,0:T(8,128)(2,1)S(1)} %bitcast.74), kind=kOutput, calls=%fused_computation.24 | convolution fusion | flops 8594128896 | bytes 25165824 | tf_op jit(solution)/shard_map/dot_general | solution.py:86
  844.9 6.3 pad_maximum_fusion.2
  (49 shorter events, 26.3 us)
Async XLA Ops:
  0.7 3.0 collective-permute-start
  24.6 135.8 %copy-start.3 = (f32[1,16,2048]{1,2,0:T(8,128)S(1)}, f32[1,16,2048]{1,2,0:T(8,128)}, u32[]{:S(2)}) copy-start(f32[1,16,2048]{1,2,0:T(8,128)} %copy.56) | copy-start | bytes 393220
  24.6 135.8 %copy-start.4 = (f32[1,16,2048]{1,2,0:T(8,128)S(1)}, f32[1,16,2048]{1,2,0:T(8,128)}, u32[]{:S(2)}) copy-start(f32[1,16,2048]{1,2,0:T(8,128)} %copy.57) | copy-start | bytes 393220
  229.9 99.2 %all-to-all-start = ((bf16[2,1024,2048]{1,0,2:T(2,128)(2,1)}), bf16[2,1024,2048]{1,0,2:T(2,128)(2,1)}, u32[]{:S(2)}, u32[]{:S(2)}) async-start(bf16[2,1024,2048]{1,0,2:T(2,128)(2,1)} %copy.47), calls=%async_computation | async-start | bytes 16777216 | tf_op jit(solution)/shard_map/all_to_all | solution.py:103
  357.2 6.9 copy-start
  357.2 11.4 %slice-start = ((s8[8388608]{0:T(1024)(128)(4,1)}), s8[4194304]{0:T(1024)(128)(4,1)S(1)}, s32[]{:S(2)}) async-start(s8[8388608]{0:T(1024)(128)(4,1)} %bitcast.67), calls=%async_computation.2 | async-start | bytes 8388608
  364.1 4.5 slice-start.1
  477.4 257.4 %all-to-all-start.1 = ((bf16[2,1024,2048]{1,0,2:T(2,128)(2,1)}), bf16[2,1024,2048]{1,0,2:T(2,128)(2,1)}, u32[]{:S(2)}, u32[]{:S(2)}) async-start(bf16[2,1024,2048]{1,0,2:T(2,128)(2,1)} %pad_maximum_fusion.1), calls=%async_computation.1 | async-start | bytes 16777216 | tf_op jit(solution)/shard_map/all_to_all | solution.py:105
  792.3 14.9 %copy-start.2 = (bf16[1,1024,2048]{2,1,0:T(8,128)(2,1)S(1)}, bf16[1,1024,2048]{2,1,0:T(8,128)(2,1)}, u32[]{:S(2)}) copy-start(bf16[1,1024,2048]{2,1,0:T(8,128)(2,1)} %copy.63) | copy-start | bytes 12582916
  792.3 28.2 %slice-start.4 = ((s8[8388608]{0:T(1024)(128)(4,1)}), s8[4194304]{0:T(1024)(128)(4,1)S(1)}, s32[]{:S(2)}) async-start(s8[8388608]{0:T(1024)(128)(4,1)} %bitcast.75), calls=%async_computation.6 | async-start | bytes 8388608
  792.3 40.4 %slice-start.2 = ((s8[8388608]{0:T(1024)(128)(4,1)}), s8[4194304]{0:T(1024)(128)(4,1)S(1)}, s32[]{:S(2)}) async-start(s8[8388608]{0:T(1024)(128)(4,1)} %bitcast.73), calls=%async_computation.4 | async-start | bytes 8388608
  807.2 13.4 %slice-start.5 = ((s8[8388608]{0:T(1024)(128)(4,1)}), s8[4194304]{0:T(1024)(128)(4,1)S(1)}, s32[]{:S(2)}) async-start(s8[8388608]{0:T(1024)(128)(4,1)} %bitcast.75), calls=%async_computation.7 | async-start | bytes 8388608
  807.2 25.5 %slice-start.3 = ((s8[8388608]{0:T(1024)(128)(4,1)}), s8[4194304]{0:T(1024)(128)(4,1)S(1)}, s32[]{:S(2)}) async-start(s8[8388608]{0:T(1024)(128)(4,1)} %bitcast.73), calls=%async_computation.5 | async-start | bytes 8388608
  820.5 12.2 %copy-start.1 = (bf16[1,1024,2048]{2,1,0:T(8,128)(2,1)S(1)}, bf16[1,1024,2048]{2,1,0:T(8,128)(2,1)}, u32[]{:S(2)}) copy-start(bf16[1,1024,2048]{2,1,0:T(8,128)(2,1)} %copy.62) | copy-start | bytes 12582916
  832.7 12.1 %copy-start.5 = (bf16[1024,2048]{1,0:T(8,128)(2,1)S(1)}, bf16[1024,2048]{1,0:T(8,128)(2,1)}, u32[]{:S(2)}) copy-start(bf16[1024,2048]{1,0:T(8,128)(2,1)} %add_convert_fusion.1) | copy-start | bytes 12582916
where the time goes:
time: 858 us; the launch traced here: 852 us
  other arithmetic  304 us (35%)
  matrix products  222 us (26%)
  local copies, waits for them, and re-layouts  203 us (24%)
  waiting for transfers between devices  95.2 us (11%)
  blocking collectives  15.4 us (2%)
  starting transfers between devices  11.6 us (1%)
    slice x1, matrix products, channelize(): outcome[:, :, :length].reshape(2, channel_count, window_count, length)  136 us
    all_to_all x1, waiting for transfers between devices, per_device(): lax.all_to_all(strips, 'tm', split_axis=2, concat_axis=2, tiled=True)  94 us
    dot_general x1, other arithmetic, second_pass(): jnp.dot(values[0], big_sin, preferred_element_type=jnp.float32)  63.3 us
    dot_general x1, other arithmetic, second_pass(): jnp.dot(values[1], big_sin, preferred_element_type=jnp.float32)  63.3 us
    dot_general x1, other arithmetic, second_pass(): jnp.dot(values[0], big_cos, preferred_element_type=jnp.float32)  62.8 us
    dot_general x1, other arithmetic, second_pass(): jnp.dot(values[1], big_cos, preferred_element_type=jnp.float32)  62.8 us
    another operation x4, local copies, waits for them, and re-layouts, first_pass(): turned = jnp.stack([turned_real, turned_imag]).astype(jnp.bfloat16)  55.5 us
    unnamed x28, local copies, waits for them, and re-layouts  47.4 us
  transfers between devices with their start and end apart: 3, of which 2 were waited for; matrix products, arithmetic and copies ran while one was open for 30% of the time, Pallas kernels for 0%

commit v1 on v0

--- a/solution.py
+++ b/solution.py
@@ -6,6 +6,12 @@
 
 K = 256
 TWO_PI = 2.0 * math.pi
+
+
+def stacked_exchange(x, name, split, join):
+    cells = jnp.split(x, lax.axis_size(name), axis=split)
+    incoming = lax.all_to_all(jnp.stack(cells), name, 0, 0)
+    return jnp.concatenate(incoming, axis=join)
 
 
 def passed_along(value, axis, steps):
@@ -100,7 +106,7 @@
     products = channelize(every_window, filters, local_chan, block_len)
     window_total = products.shape[2]
     strips = products.reshape(2, local_chan * window_total, block_len)
-    partial_sums = first_pass(lax.all_to_all(strips, "tm", split_axis=2, concat_axis=2, tiled=True))
+    partial_sums = first_pass(stacked_exchange(strips, "tm", 2, 2))
     finished = second_pass(
         lax.all_to_all(partial_sums, "tm", split_axis=2, concat_axis=2, tiled=True)
     )

time: 858 us -> 817 us (0.952)
  local copies, waits for them, and re-layouts: 203 us -> 156 us
    another operation x3 -> x2, local copies, waits for them, and re-layouts: 45.5 us -> 24 us
    slice x1 -> x0, local copies, waits for them, and re-layouts: 17.4 us -> none  [first_pass(): grouped[0]]
    squeeze x2 -> x0, local copies, waits for them, and re-layouts: 14.1 us -> none  [the longest x1 7.15 us: first_pass(): grouped[1]]
    all_to_all x0 -> x1, local copies, waits for them, and re-layouts: none -> 11.6 us  [stacked_exchange(): incoming = lax.all_to_all(jnp.stack(cells), name, 0, 0)]
    unnamed x3 -> x9, other arithmetic: 0.01 us -> 9.11 us
    unnamed x28 -> x26, local copies, waits for them, and re-layouts: 47.4 us -> 41.8 us
  transfers between devices with their start and end apart: 3 -> 3, of which waited for: 2 -> 2; matrix products, arithmetic and copies ran while one was open for 30% -> 31% of each run, Pallas kernels for 0% -> 0%
where the time goes in v1:
time: 817 us; the launch traced here: 811 us
  other arithmetic  307 us (38%)
  matrix products  227 us (28%)
  local copies, waits for them, and re-layouts  156 us (19%)
  waiting for transfers between devices  95.2 us (12%)
  blocking collectives  15.4 us (2%)
  starting transfers between devices  11.4 us (1%)
    slice x1, matrix products, channelize(): outcome[:, :, :length].reshape(2, channel_count, window_count, length)  144 us
    all_to_all x1, waiting for transfers between devices, stacked_exchange(): incoming = lax.all_to_all(jnp.stack(cells), name, 0, 0)  94 us
    dot_general x1, other arithmetic, second_pass(): jnp.dot(values[0], big_sin, preferred_element_type=jnp.float32)  63.3 us
    dot_general x1, other arithmetic, second_pass(): jnp.dot(values[1], big_sin, preferred_element_type=jnp.float32)  63.3 us
    dot_general x1, other arithmetic, second_pass(): jnp.dot(values[0], big_cos, preferred_element_type=jnp.float32)  62.8 us
    dot_general x1, other arithmetic, second_pass(): jnp.dot(values[1], big_cos, preferred_element_type=jnp.float32)  62.8 us
    another operation x4, local copies, waits for them, and re-layouts, first_pass(): turned = jnp.stack([turned_real, turned_imag]).astype(jnp.bfloat16)  55.6 us
    unnamed x26, local copies, waits for them, and re-layouts  41.8 us
  transfers between devices with their start and end apart: 3, of which 2 were waited for; matrix products, arithmetic and copies ran while one was open for 31% of the time, Pallas kernels for 0%

profile of v1, /device:TPU:0, one launch (start us, length us, event | category | flops | bytes accessed | tf_op | source)
XLA Modules:
  0.0 811.4 jit_solution(144018718931603277)
XLA Ops:
  4.6 15.4 %all_gather.3 = bf16[2,16,2304]{2,0,1:T(2,128)(2,1)S(1)} all-gather(bf16[2,4,2304]{2,0,1:T(2,128)(2,1)S(1)} %copy.142), channel_id=1, replica_groups=mesh['tm'=8,'strip'=4] {'strip'}, dimensions={1}, use_global_device_ids=true | all-gather | bytes 184320 | tf_op jit(solution)/shard_map/all_gather | solution.py:103
  20.0 1.6 copy.143
  24.6 144.3 %fusion.104 = f32[128,16,2048]{0,1,2:T(8,128)S(1)} fusion(bf16[2,16,2304]{1,0,2:T(2,128)(2,1)S(1)} %copy.143, bf16[128,2,256]{0,1,2:T(2,128)(2,1)S(1)} %copy.144), kind=kOutput, calls=%fused_computation.156 | convolution fusion | flops 4294967296 | bytes 17055744 | tf_op jit(solution)/shard_map/slice | solution.py:52
  169.0 16.4 %add_convert_fusion = (bf16[64,16,2048]{0,1,2:T(8,128)(2,1)}, bf16[64,16,2048]{0,1,2:T(8,128)(2,1)}) fusion(f32[128,16,2048]{0,1,2:T(8,128)S(1)} %fusion.104, f32[16,2048]{0,1:T(8,128)S(1)} %bitcast.117, f32[16,2048]{0,1:T(8,128)S(1)} %bitcast.116), kind=kLoop, calls=%fused_computation.11 | loop fusion | flops 16777216 | bytes 25427968 | tf_op jit(solution)/shard_map/convert.11
  185.4 12.0 %copy.147 = bf16[64,16,2048]{2,1,0:T(8,128)(2,1)} copy(bf16[64,16,2048]{0,1,2:T(8,128)(2,1)} %get-tuple-element.7) | data formatting | bytes 8388608 | tf_op jit(solution)/shard_map/convert.11
  197.4 12.0 %copy.148 = bf16[64,16,2048]{2,1,0:T(8,128)(2,1)} copy(bf16[64,16,2048]{0,1,2:T(8,128)(2,1)} %get-tuple-element.8) | data formatting | bytes 8388608 | tf_op jit(solution)/shard_map/convert.10
  209.4 2.4 bitcast_dynamic-update-slice_fusion.6
  221.4 5.2 all-to-all-start
  226.6 94.0 %all-to-all-done = bf16[8,2,1024,256]{3,2,1,0:T(8,128)(2,1)} async-done(((bf16[8,2,1024,256]{3,2,1,0:T(8,128)(2,1)}), bf16[8,2,1024,256]{3,2,1,0:T(8,128)(2,1)}, u32[]{:S(2)}, u32[]{:S(2)}) %all-to-all-start) | async-done | bytes 8388640 | tf_op jit(solution)/shard_map/all_to_all | solution.py:13
  320.6 11.6 %copy.161 = bf16[8,2,1024,256]{3,0,2,1:T(8,128)(2,1)} copy(bf16[8,2,1024,256]{3,2,1,0:T(8,128)(2,1)} %all-to-all-done) | data formatting | bytes 16777216 | tf_op jit(solution)/shard_map/all_to_all | solution.py:13
  332.2 6.9 fusion.18
  339.1 4.7 fusion.19
  343.7 4.5 fusion.21
  348.2 13.6 %fusion.7 = (bf16[1024,8,256]{2,1,0:T(8,128)(2,1)}, bf16[1024,8,256]{2,1,0:T(8,128)(2,1)}) fusion(f32[8,256]{1,0:T(8,128)S(1)} %get-tuple-element.17, f32[8,256]{1,0:T(8,128)S(1)} %get-tuple-element.16, f32[1024,256,8]{1,2,0:T(8,128)} %fusion.18, f32[1024,256,8]{1,2,0:T(8,128)} %fusion.19, f32[1024,256,8]{1,2,0:T(8,128)} %fusion.21, ...), kind=kOutput, calls=%fused_computation.32 | convolution fusion | flops 54526976 | bytes 37765120 | tf_op jit(solution)/shard_map/qn,rns->rqs/dot_general | solution.py:72
  361.9 7.4 stack.80
  369.2 20.6 %copy.150 = bf16[1,1024,2048]{1,0,2:T(2,128)(2,1)} copy(bf16[1,1024,2048]{2,1,0:T(8,128)(2,1)} %stack.80) | data formatting | bytes 8388608 | tf_op jit(solution)/shard_map/stack | solution.py:79
  389.9 7.4 stack.81
  397.2 20.3 %copy.151 = bf16[1,1024,2048]{1,0,2:T(2,128)(2,1)} copy(bf16[1,1024,2048]{2,1,0:T(8,128)(2,1)} %stack.81) | data formatting | bytes 8388608 | tf_op jit(solution)/shard_map/stack | solution.py:79
  417.5 20.0 %pad_maximum_fusion = bf16[2,1024,2048]{1,0,2:T(2,128)(2,1)} fusion(bf16[1,1024,2048]{1,0,2:T(2,128)(2,1)} %copy.151, bf16[1,1024,2048]{1,0,2:T(2,128)(2,1)} %copy.150), kind=kLoop, calls=%fused_computation.27 | loop fusion | flops 16777216 | bytes 16777216 | tf_op jit(solution)/shard_map/stack | solution.py:79
  437.5 5.0 all-to-all-start.1
  442.5 62.8 %multiply_convert_fusion.22 = bf16[2048,2048]{1,0:T(8,128)(2,1)} fusion(), kind=kLoop, calls=%fused_computation.7.clone.1.clone | loop fusion | flops 67108864 | bytes 8388608 | tf_op jit(solution)/shard_map/dot_general | solution.py:89
  505.3 63.3 %multiply_convert_fusion.20 = bf16[2048,2048]{1,0:T(8,128)(2,1)} fusion(), kind=kLoop, calls=%fused_computation.6.clone.1.clone.clone.clone.1 | loop fusion | flops 67108864 | bytes 8388608 | tf_op jit(solution)/shard_map/dot_general | solution.py:89
  568.6 62.8 %multiply_convert_fusion.21 = bf16[2048,2048]{1,0:T(8,128)(2,1)} fusion(), kind=kLoop, calls=%fused_computation.7.clone.clone.1 | loop fusion | flops 67108864 | bytes 8388608 | tf_op jit(solution)/shard_map/dot_general | solution.py:92
  631.4 63.3 %multiply_convert_fusion.19 = bf16[2048,2048]{1,0:T(8,128)(2,1)} fusion(), kind=kLoop, calls=%fused_computation.6.clone.clone.clone.clone.1 | loop fusion | flops 67108864 | bytes 8388608 | tf_op jit(solution)/shard_map/dot_general | solution.py:92
  694.7 17.5 %fusion.102 = (bf16[1,1024,2048]{1,0,2:T(2,128)(2,1)}, bf16[1,1024,2048]{1,0,2:T(2,128)(2,1)}) fusion(bf16[2,1024,2048]{1,0,2:T(2,128)(2,1)} %all-to-all-done.1), kind=kLoop, calls=%fused_computation.154 | loop fusion | bytes 16777216 | tf_op jit(solution)/shard_map/slice | solution.py:89
  712.2 20.1 %copy.158 = bf16[1,1024,2048]{2,1,0:T(8,128)(2,1)} copy(bf16[1,1024,2048]{1,0,2:T(2,128)(2,1)} %get-tuple-element.9) | data formatting | bytes 8388608
  732.3 19.8 %copy.159 = bf16[1,1024,2048]{2,1,0:T(8,128)(2,1)} copy(bf16[1,1024,2048]{1,0,2:T(2,128)(2,1)} %get-tuple-element.10) | data formatting | bytes 8388608
  752.2 14.9 %fusion.11 = f32[1024,2048]{1,0:T(8,128)} fusion(bf16[1,1024,2048]{2,1,0:T(8,128)(2,1)} %copy.158, bf16[2048,2048]{1,0:T(8,128)(2,1)} %multiply_convert_fusion.22), kind=kOutput, calls=%fused_computation.41 | convolution fusion | flops 8589934592 | bytes 20971520 | tf_op jit(solution)/shard_map/dot_general | solution.py:89
  767.1 13.3 %fusion.10 = f32[1024,2048]{1,0:T(8,128)} fusion(bf16[1,1024,2048]{2,1,0:T(8,128)(2,1)S(1)} %copy-done.4, bf16[2048,2048]{1,0:T(8,128)(2,1)} %multiply_convert_fusion.21), kind=kOutput, calls=%fused_computation.40 | convolution fusion | flops 8589934592 | bytes 20971520 | tf_op jit(solution)/shard_map/dot_general | solution.py:92
  780.5 12.2 %add_convert_fusion.1 = bf16[1024,2048]{1,0:T(8,128)(2,1)} fusion(f32[1024,2048]{1,0:T(8,128)} %fusion.11, bf16[1,1024,2048]{2,1,0:T(8,128)(2,1)S(1)} %copy-done.4, bf16[2048,2048]{1,0:T(8,128)(2,1)S(1)} %bitcast.115), kind=kOutput, calls=%fused_computation.39 | convolution fusion | flops 8594128896 | bytes 25165824 | tf_op jit(solution)/shard_map/dot_general | solution.py:89
  792.7 12.1 %subtract_convert_fusion.1 = bf16[1024,2048]{1,0:T(8,128)(2,1)} fusion(f32[1024,2048]{1,0:T(8,128)} %fusion.10, bf16[1,1024,2048]{2,1,0:T(8,128)(2,1)S(1)} %copy-done.3, bf16[2048,2048]{1,0:T(8,128)(2,1)S(1)} %bitcast.113), kind=kOutput, calls=%fused_computation.38 | convolution fusion | flops 8594128896 | bytes 25165824 | tf_op jit(solution)/shard_map/dot_general | solution.py:92
  804.8 6.3 pad_maximum_fusion.1
  (50 shorter events, 17.2 us)
Async XLA Ops:
  0.7 3.0 collective-permute-start
  24.6 144.3 %copy-start.5 = (f32[1,16,2048]{1,2,0:T(8,128)S(1)}, f32[1,16,2048]{1,2,0:T(8,128)}, u32[]{:S(2)}) copy-start(f32[1,16,2048]{1,2,0:T(8,128)} %copy.156) | copy-start | bytes 393220
  24.6 144.3 %copy-start.6 = (f32[1,16,2048]{1,2,0:T(8,128)S(1)}, f32[1,16,2048]{1,2,0:T(8,128)}, u32[]{:S(2)}) copy-start(f32[1,16,2048]{1,2,0:T(8,128)} %copy.157) | copy-start | bytes 393220
  209.4 2.9 copy-start
  209.4 4.2 copy-start.1
  221.4 99.2 %all-to-all-start = ((bf16[8,2,1024,256]{3,2,1,0:T(8,128)(2,1)}), bf16[8,2,1024,256]{3,2,1,0:T(8,128)(2,1)}, u32[]{:S(2)}, u32[]{:S(2)}) async-start(bf16[8,2,1024,256]{3,2,1,0:T(8,128)(2,1)} %fusion.34), calls=%async_computation | async-start | bytes 16777216 | tf_op jit(solution)/shard_map/all_to_all | solution.py:13
  332.2 6.9 copy-start.2
  437.5 257.2 %all-to-all-start.1 = ((bf16[2,1024,2048]{1,0,2:T(2,128)(2,1)}), bf16[2,1024,2048]{1,0,2:T(2,128)(2,1)}, u32[]{:S(2)}, u32[]{:S(2)}) async-start(bf16[2,1024,2048]{1,0,2:T(2,128)(2,1)} %pad_maximum_fusion), calls=%async_computation.1 | async-start | bytes 16777216 | tf_op jit(solution)/shard_map/all_to_all | solution.py:111
  752.2 14.9 %copy-start.4 = (bf16[1,1024,2048]{2,1,0:T(8,128)(2,1)S(1)}, bf16[1,1024,2048]{2,1,0:T(8,128)(2,1)}, u32[]{:S(2)}) copy-start(bf16[1,1024,2048]{2,1,0:T(8,128)(2,1)} %copy.159) | copy-start | bytes 12582916
  752.2 28.3 %slice-start.2 = ((s8[8388608]{0:T(1024)(128)(4,1)}), s8[4194304]{0:T(1024)(128)(4,1)S(1)}, s32[]{:S(2)}) async-start(s8[8388608]{0:T(1024)(128)(4,1)} %bitcast.114), calls=%async_computation.4 | async-start | bytes 8388608
  752.2 40.4 %slice-start = ((s8[8388608]{0:T(1024)(128)(4,1)}), s8[4194304]{0:T(1024)(128)(4,1)S(1)}, s32[]{:S(2)}) async-start(s8[8388608]{0:T(1024)(128)(4,1)} %bitcast.112), calls=%async_computation.2 | async-start | bytes 8388608
  767.1 13.4 %slice-start.3 = ((s8[8388608]{0:T(1024)(128)(4,1)}), s8[4194304]{0:T(1024)(128)(4,1)S(1)}, s32[]{:S(2)}) async-start(s8[8388608]{0:T(1024)(128)(4,1)} %bitcast.114), calls=%async_computation.5 | async-start | bytes 8388608
  767.1 25.5 %slice-start.1 = ((s8[8388608]{0:T(1024)(128)(4,1)}), s8[4194304]{0:T(1024)(128)(4,1)S(1)}, s32[]{:S(2)}) async-start(s8[8388608]{0:T(1024)(128)(4,1)} %bitcast.112), calls=%async_computation.3 | async-start | bytes 8388608
  780.5 12.2 %copy-start.3 = (bf16[1,1024,2048]{2,1,0:T(8,128)(2,1)S(1)}, bf16[1,1024,2048]{2,1,0:T(8,128)(2,1)}, u32[]{:S(2)}) copy-start(bf16[1,1024,2048]{2,1,0:T(8,128)(2,1)} %copy.158) | copy-start | bytes 12582916
  792.7 12.2 %copy-start.7 = (bf16[1024,2048]{1,0:T(8,128)(2,1)S(1)}, bf16[1024,2048]{1,0:T(8,128)(2,1)}, u32[]{:S(2)}) copy-start(bf16[1024,2048]{1,0:T(8,128)(2,1)} %add_convert_fusion.1) | copy-start | bytes 12582916
